TPU v7x, 32 devices: a whole 2x2x4 slice. The times are simulated.
32 devices in a mesh: ctx: 4 (over y, x), head: 8 (over z, core).
Axes of the slice: x: 2, y: 2, z: 4, core: 2. Of those that a mesh axis runs over, the one named last changes fastest.
Arguments:
- pooled_q: bfloat16 [2, 512, 4096], P(None, 'ctx', 'head'), may hold values from -240 to 240
- pooled_k: bfloat16 [2, 512, 8, 384], P(None, 'ctx'), may hold values from -9.5 to 9.5
- wq: bfloat16 [32, 128, 128], P('head'), may hold values from -0.5 to 0.5
- wk: bfloat16 [8, 384, 128], replicated, may hold values from -0.3125 to 0.3125
- teacher: bfloat16 [2, 32, 512, 512], P(None, 'head', 'ctx'), may hold values from 9.9658966e-05 to 1
- doc_ids: int32 [2, 512], P(None, 'ctx'), may hold values from 0 to 3, never falling along the last dimension, each value on 1 to 256 neighbouring positions
- owner_rows: int32 [512], P('ctx'), may hold values from 0 to 511, as said below
Outputs:
- wq_grad: float32 [32, 128, 128], P('head')
- wk_grad: float32 [3072, 128], P('head')
- row_kl: float32 [2, 32, 512], P(None, 'head', 'ctx')
Inputs may be any that keep to these rules, and one draw needn't show every extreme that they name: `owner_rows`: slots of each ctx index hold rising block rows, exactly 128 / 4 of them from each aligned range of 128 rows; every row appears once.
All inputs are finite; a program needn't handle non-finite values.
Results may differ from a plain program's by a relative error of at most 0.0034.
The roundings to bfloat16 on the way count: a program that leaves them out, or rounds other values in their place, can miss the bound.
Values may be sent and summed in bfloat16 or wider, within the bound.
A program may use at most 64 MiB of HBM per device.

v0:
```python
import math

import jax
import jax.numpy as jnp
from jax import lax
from jax.sharding import PartitionSpec as P

NEG_FILL = -1e30


def local(pooled_q, pooled_k, wq, wk, teacher, doc_ids, owner_rows):
    seqs, rows, width = pooled_q.shape
    local_heads, head_dim, gate_dim = wq.shape
    kv_heads, features, unused_dim = wk.shape
    blocks = teacher.shape[3]
    me_ctx = lax.axis_index("ctx")
    head_base = lax.axis_index("head") * local_heads
    group = lax.axis_size("head") * local_heads // kv_heads
    scale = 1.0 / math.sqrt(gate_dim)
    tile = min(512, blocks)
    span = min(128, rows)
    kv_index = [(head_base + hl) // group for hl in range(local_heads)]
    key_feats = []
    key_parts = []
    for hl in range(local_heads):
        feats = lax.dynamic_index_in_dim(pooled_k, kv_index[hl], 2, keepdims=False)
        w_sel = lax.dynamic_index_in_dim(wk, kv_index[hl], 0, keepdims=False)
        key_feats.append(feats)
        key_parts.append(
            jnp.einsum("srf,fe->sre", feats, w_sel, preferred_element_type=jnp.float32).astype(
                jnp.bfloat16
            )
        )
    key_local = jnp.stack(key_parts, 2)
    key_all = lax.all_gather(key_local, "ctx", axis=1, tiled=True)
    doc_all = lax.all_gather(doc_ids, "ctx", axis=1, tiled=True)
    row_ids = me_ctx * rows + jnp.arange(rows, dtype=jnp.int32)
    row_docs = jnp.take(doc_all, row_ids, axis=1)
    queries = pooled_q.reshape(seqs, rows, local_heads, head_dim)
    query_gate = jnp.einsum(
        "srhd,hde->srhe", queries, wq, preferred_element_type=jnp.float32
    ).astype(jnp.bfloat16)
    grad_key_parts = []
    grad_query_parts = []
    loss_parts = []
    for hl in range(local_heads):
        keys = key_all[:, :, hl]
        grad_keys = jnp.zeros((seqs, blocks, gate_dim), jnp.float32)
        q_rows = query_gate[:, 0:span, hl]
        r_ids = row_ids
        r_docs = row_docs
        t_rows = teacher[:, hl, 0:span]
        count = jnp.max(r_ids) // tile + 1

        def scores_at(index, q_rows=q_rows, r_ids=r_ids, r_docs=r_docs, t_rows=t_rows, keys=keys):
            col = index * tile
            k_tile = lax.dynamic_slice_in_dim(keys, col, tile, 1)
            raw = scale * jnp.einsum(
                "sgd,skd->sgk", q_rows, k_tile, preferred_element_type=jnp.float32
            )
            cols = col + jnp.arange(tile, dtype=jnp.int32)
            d_tile = lax.dynamic_slice_in_dim(doc_all, col, tile, 1)
            allowed = (cols[None, None, :] <= r_ids[None, :, None]) & (
                d_tile[:, None, :] == r_docs[:, :, None]
            )
            tch = lax.dynamic_slice_in_dim(t_rows, col, tile, 2).astype(jnp.float32)
            return (k_tile, raw, allowed, tch)

        def first_pass(index, carry, scores_at=scores_at):
            top, total, mass, entropy, cross = carry
            k_tile, raw, allowed, tch = scores_at(index)
            new_top = jnp.maximum(top, jnp.max(jnp.where(allowed, raw, NEG_FILL), axis=2))
            shifted = jnp.where(allowed, raw - new_top[:, :, None], 0.0)
            total = total * jnp.exp(top - new_top) + jnp.sum(
                jnp.where(allowed, jnp.exp(shifted), 0.0), axis=2
            )
            mass = mass + jnp.sum(jnp.where(allowed, tch, 0.0), axis=2)
            entropy = entropy + jnp.sum(jnp.where(allowed, tch * jnp.log(tch), 0.0), axis=2)
            cross = cross + jnp.sum(jnp.where(allowed, tch * raw, 0.0), axis=2)
            return (new_top, total, mass, entropy, cross)

        zeros_rows = jnp.zeros((seqs, q_rows.shape[1]), jnp.float32)
        start_stats = (zeros_rows + NEG_FILL, zeros_rows, zeros_rows, zeros_rows, zeros_rows)
        top, total, mass, entropy, cross = lax.fori_loop(0, count, first_pass, start_stats)
        loss_pieces = entropy / mass - jnp.log(mass) - cross / mass + top + jnp.log(total)

        def second_pass(
            index, carry, scores_at=scores_at, top=top, total=total, mass=mass, q_rows=q_rows
        ):
            grad_rows, grad_all = carry
            k_tile, raw, allowed, tch = scores_at(index)
            shifted = jnp.where(allowed, raw - top[:, :, None], 0.0)
            probs = jnp.where(allowed, jnp.exp(shifted) / total[:, :, None], 0.0)
            target = jnp.where(allowed, tch / mass[:, :, None], 0.0)
            diff = (probs - target).astype(jnp.bfloat16)
            grad_rows = grad_rows + jnp.einsum(
                "sgk,skd->sgd", diff, k_tile, preferred_element_type=jnp.float32
            )
            col = index * tile
            current = lax.dynamic_slice_in_dim(grad_all, col, tile, 1)
            update = current + jnp.einsum(
                "sgk,sgd->skd", diff, q_rows, preferred_element_type=jnp.float32
            )
            grad_all = lax.dynamic_update_slice_in_dim(grad_all, update, col, 1)
            return (grad_rows, grad_all)

        grad_rows0 = jnp.zeros((seqs, q_rows.shape[1], gate_dim), jnp.float32)
        grad_rows, grad_keys = lax.fori_loop(0, count, second_pass, (grad_rows0, grad_keys))
        query_pieces = (scale * grad_rows).astype(jnp.bfloat16)
        grad_key_parts.append(grad_keys)
        grad_query_parts.append(query_pieces)
        loss_parts.append(loss_pieces)
    grad_key_all = jnp.stack(grad_key_parts, 2)
    grad_key_own = lax.psum_scatter(grad_key_all, "ctx", scatter_dimension=1, tiled=True)
    grad_key_own = (scale * grad_key_own).astype(jnp.bfloat16)
    grad_query = jnp.stack(grad_query_parts, 2)
    wq_term = jnp.einsum("srhd,srhe->hde", queries, grad_query, preferred_element_type=jnp.float32)
    wk_terms = jnp.stack(
        [
            jnp.einsum(
                "srf,sre->fe",
                key_feats[hl],
                grad_key_own[:, :, hl],
                preferred_element_type=jnp.float32,
            )
            for hl in range(local_heads)
        ],
        0,
    )
    wq_total, wk_total = lax.psum((wq_term, wk_terms), "ctx")
    whole = jnp.zeros((features, kv_heads, gate_dim), jnp.float32)
    for hl in range(local_heads):
        current = lax.dynamic_index_in_dim(whole, kv_index[hl], 1, keepdims=False)
        whole = lax.dynamic_update_index_in_dim(whole, current + wk_total[hl], kv_index[hl], 1)
    wk_grad = lax.psum_scatter(
        whole.reshape(features * kv_heads, gate_dim), "head", scatter_dimension=0, tiled=True
    )
    losses = jnp.stack(loss_parts, 1)
    all_losses = lax.all_gather(losses, "ctx", axis=2, tiled=True)
    row_kl = jnp.take(all_losses, owner_rows, axis=2)
    return (wq_total, wk_grad, row_kl)


def solution(mesh):
    placed = (
        P(None, "ctx", "head"),
        P(None, "ctx", None, None),
        P("head", None, None),
        P(),
        P(None, "head", "ctx", None),
        P(None, "ctx"),
        P("ctx"),
    )
    return jax.shard_map(
        local,
        mesh=mesh,
        in_specs=placed,
        out_specs=(P("head", None, None), P("head", None), P(None, "head", "ctx")),
        check_vma=False,
    )
```

profile of v0, /device:TPU:0, one launch (start us, length us, event | category | flops | bytes accessed | tf_op | source)
XLA Modules:
  0.0 203.8 jit_solution(7175342210939709193)
XLA Ops:
  7.3 5.2 %constant_dynamic-slice_fusion.3 = (bf16[2,128,1,384]{3,2,1,0:T(2,128)(2,1)S(1)}, bf16[2,128,1,384]{3,2,1,0:T(2,128)(2,1)S(1)}, bf16[2,128,1,384]{3,2,1,0:T(2,128)(2,1)S(1)}, bf16[2,128,1,384]{3,2,1,0:T(2,128)(2,1)S(1)}) fusion(bf16[2,128,8,384]{3,2,1,0:T(8,128)(2,1)} %param.24, s32[]{:T(128)S(6)} %select_n.222, s32[]{:T(128)S(6)} %select_n.226, ...), kind=kLoop, calls=%fused_computation.221 | loop fusion | bytes 1572880 | tf_op jit(solution)/shard_map/jit(dynamic_index_in_dim)/dynamic_slice | solution.py:26
  13.6 0.7 pad_maximum_fusion.2
  17.8 11.7 %all_gather.9 = s32[2,512]{0,1:T(8,128)S(1)} all-gather(s32[2,128]{0,1:T(8,128)S(1)} %copy.197), channel_id=1, replica_groups=mesh['ctx'=4,'head'=8] {'ctx'}, dimensions={1}, use_global_device_ids=true | all-gather | bytes 5120 | tf_op jit(solution)/shard_map/all_gather | solution.py:36
  32.5 2.0 slice_bitcast_fusion.7
  34.5 10.0 %all-gather.2.cloned.1.call-done = bf16[2,512,4,128]{3,1,0,2:T(8,128)(2,1)} async-done(((bf16[2,128,4,128]{3,1,0,2:T(8,128)(2,1)}), bf16[2,512,4,128]{3,1,0,2:T(8,128)(2,1)}) %all-gather.2.cloned.1.call-update) | async-done | bytes 1048592 | tf_op jit(solution)/shard_map/all_gather | solution.py:35
  44.4 1.3 slice_bitcast_fusion.3
  45.8 1.2 while.132
  47.6 1.1 while.133
  49.3 1.2 while.134
  51.0 2.5 %while.135 = (s32[]{:T(128)}, f32[2,128,128]{2,1,0:T(8,128)S(1)}, f32[2,512,128]{2,1,0:T(8,128)S(1)}, s32[]{:T(128)}, s32[2,512]{1,0:T(2,128)S(1)}, /*index=5*/s...) while((s32[]{:T(128)}, f32[2,128,128]{2,1,0:T(8,128)S(1)}, ...), condition=%wide.region_36.37_spmd.clone, body=%wide.region_35.36_spmd.clone.sunk | while | flops 102466176 | bytes 3175705 | solution.py:108
  51.7 1.1 fusion.220
  54.2 3.0 %while.128 = (s32[]{:T(128)}, f32[2,128]{1,0:T(2,128)S(1)}, f32[2,128]{1,0:T(2,128)S(1)}, f32[2,128]{1,0:T(2,128)S(1)}, f32[2,128]{1,0:T(2,128)S(1)}, /*index=5*...) while((s32[]{:T(128)}, f32[2,128]{1,0:T(2,128)S(1)}, ...), condition=%wide.region_7.8_spmd.clone, body=%wide.region_1.7_spmd.clone.sunk | while | flops 36242560 | bytes 1876137 | solution.py:84
  54.4 1.2 select_reduce_fusion.12
  55.5 1.6 fusion.183
  57.9 2.9 %while.129 = (s32[]{:T(128)}, f32[2,128,128]{2,1,0:T(8,128)S(1)}, f32[2,512,128]{2,1,0:T(8,128)S(1)}, s32[]{:T(128)}, s32[2,512]{1,0:T(2,128)S(1)}, /*index=5*/s...) while((s32[]{:T(128)}, f32[2,128,128]{2,1,0:T(8,128)S(1)}, ...), condition=%wide.region_9.10_spmd.clone, body=%wide.region_8.9_spmd.clone.sunk | while | flops 102466176 | bytes 3159209 | solution.py:108
  58.0 1.4 fusion.190
  59.6 1.2 convolution_add_fusion.17
  61.5 1.2 while.130
  64.0 2.4 %while.131 = (s32[]{:T(128)}, f32[2,128,128]{2,1,0:T(8,128)}, f32[2,512,128]{2,1,0:T(8,128)S(1)}, s32[]{:T(128)}, s32[2,512]{1,0:T(2,128)S(1)}, /*index=5*/s32[2...) while((s32[]{:T(128)}, f32[2,128,128]{2,1,0:T(8,128)}, ...), condition=%wide.region_18.19_spmd.clone, body=%wide.region_17.18_spmd.clone.sunk | while | flops 102466176 | bytes 4470013 | solution.py:108
  64.2 1.3 fusion.200
  66.4 1.5 pad_maximum_fusion
  69.2 0.9 convolution_bitcast_fusion
  70.1 33.1 %reduce-scatter.3.cloned.1.call-done = f32[2,128,4,128]{3,1,0,2:T(8,128)} async-done(((f32[2,512,4,128]{3,1,0,2:T(8,128)}), f32[2,128,4,128]{3,1,0,2:T(8,128)}) %reduce-scatter.3.cloned.1.call-update) | async-done | bytes 524304 | tf_op jit(solution)/shard_map/reduce_scatter | solution.py:114
  103.2 1.1 multiply_convert_fusion
  105.4 1.0 pad_maximum_fusion.1
  106.5 52.9 %all-reduce.3.cloned.1.call-done = (f32[4,128,128]{1,2,0:T(8,128)}, f32[4,384,128]{2,1,0:T(8,128)}) async-done(((f32[4,128,128]{1,2,0:T(8,128)}, f32[4,384,128]{2,1,0:T(8,128)}), (f32[4,128,128]{1,2,0:T(8,128)}, f32[4,384,128]{2,1,0:T(8,128)})) %all-reduce.3.cloned.1.call-update) | async-done | bytes 1048592 | tf_op jit(solution)/shard_map/psum | solution.py:130
  159.5 1.0 copy-done.18
  160.7 2.1 %copy.291 = f32[384,8,128]{2,1,0:T(8,128)} copy(f32[384,8,128]{2,0,1:T(8,128)S(1)} %fusion.81) | data formatting | bytes 3145728 | tf_op jit(solution)/shard_map/jit(dynamic_update_index_in_dim)/dynamic_update_slice | solution.py:134
  163.7 8.0 %all_gather.11 = f32[2,4,512]{2,1,0:T(4,128)S(1)} all-gather(f32[2,4,128]{2,1,0:T(4,128)S(1)} %pad_maximum_fusion.3), channel_id=1, replica_groups=mesh['ctx'=4,'head'=8] {'ctx'}, dimensions={2}, use_global_device_ids=true | all-gather | bytes 20480 | tf_op jit(solution)/shard_map/all_gather | solution.py:139
  172.0 0.7 gather_fusion.1
  173.7 0.8 copy.247
  174.5 22.7 %reduce-scatter.5.cloned.1.call-done = f32[384,128]{1,0:T(8,128)} async-done(((f32[3072,128]{1,0:T(8,128)}), f32[384,128]{1,0:T(8,128)}) %reduce-scatter.5.cloned.1.call-update) | async-done | bytes 196624 | tf_op jit(solution)/shard_map/reduce_scatter | solution.py:135
  (272 shorter events, 21.3 us)
Async XLA Ops:
  7.2 5.3 %copy-start = (bf16[8,384,128]{2,1,0:T(8,128)(2,1)S(1)}, bf16[8,384,128]{2,1,0:T(8,128)(2,1)}, u32[]{:S(2)}) copy-start(bf16[8,384,128]{2,1,0:T(8,128)(2,1)} %param.26) | copy-start | bytes 2359300
  7.2 37.3 %all-gather.2.cloned.1.call-start = ((), (), s32[]{:S(2)}) async-start(), calls=%async_computation.2 | async-start | bytes 1310720 | tf_op jit(solution)/shard_map/all_gather | solution.py:35
  12.4 0.8 copy-start.10
  12.4 1.0 copy-start.12
  12.5 1.0 copy-start.14
  12.5 1.1 copy-start.16
  12.5 5.2 %copy-start.63 = (s32[2,128]{1,0:T(2,128)S(1)}, s32[2,128]{1,0:T(2,128)}, u32[]{:S(2)}) copy-start(s32[2,128]{1,0:T(2,128)} %param.28) | copy-start | bytes 3076
  12.5 18.0 %copy-start.19 = (bf16[2,128,512]{2,1,0:T(8,128)(2,1)S(1)}, bf16[2,128,512]{2,1,0:T(8,128)(2,1)}, u32[]{:S(2)}) copy-start(bf16[2,128,512]{2,1,0:T(8,128)(2,1)} %param.23) | copy-start | bytes 786436
  12.5 17.9 %copy-start.22 = (bf16[4,128,128]{2,1,0:T(8,128)(2,1)S(1)}, bf16[4,128,128]{2,1,0:T(8,128)(2,1)}, u32[]{:S(2)}) copy-start(bf16[4,128,128]{2,1,0:T(8,128)(2,1)} %param.25) | copy-start | bytes 393220
  14.3 88.9 %reduce-scatter.3.cloned.1.call-start = ((), (), s32[]{:S(2)}) async-start(), calls=%async_computation.3 | async-start | bytes 2621440 | tf_op jit(solution)/shard_map/reduce_scatter | solution.py:114
  57.9 3.0 %copy-start.8 = (bf16[2,128,128]{2,1,0:T(8,128)(2,1)S(1)}, bf16[2,128,128]{2,1,0:T(8,128)(2,1)}, u32[]{:S(2)}) copy-start(bf16[2,128,128]{2,1,0:T(8,128)(2,1)} %copy.218) | copy-start | bytes 196612
  64.1 1.3 copy-start.5
  64.2 1.6 copy-start.9
  67.9 0.9 copy-start.2
  67.9 1.0 copy-start.4
  67.9 1.1 copy-start.7
  67.9 1.3 copy-start.20
  67.9 91.5 %all-reduce.3.cloned.1.call-start = ((), (), s32[]{:S(2)}) async-start(), calls=%async_computation.5 | async-start | bytes 2097152 | tf_op jit(solution)/shard_map/psum | solution.py:130
  69.0 35.3 %copy-start.17 = (bf16[2,128,1,384]{3,2,1,0:T(2,128)(2,1)S(1)}, bf16[2,128,1,384]{3,2,1,0:T(2,128)(2,1)}, u32[]{:S(2)}) copy-start(bf16[2,128,1,384]{3,2,1,0:T(2,128)(2,1)} %copy-done.16) | copy-start | bytes 589828
  69.2 35.5 %copy-start.15 = (bf16[2,128,1,384]{3,2,1,0:T(2,128)(2,1)S(1)}, bf16[2,128,1,384]{3,2,1,0:T(2,128)(2,1)}, u32[]{:S(2)}) copy-start(bf16[2,128,1,384]{3,2,1,0:T(2,128)(2,1)} %copy-done.14) | copy-start | bytes 589828
  69.2 35.7 %copy-start.13 = (bf16[2,128,1,384]{3,2,1,0:T(2,128)(2,1)S(1)}, bf16[2,128,1,384]{3,2,1,0:T(2,128)(2,1)}, u32[]{:S(2)}) copy-start(bf16[2,128,1,384]{3,2,1,0:T(2,128)(2,1)} %copy-done.12) | copy-start | bytes 589828
  69.2 35.9 %copy-start.11 = (bf16[2,128,1,384]{3,2,1,0:T(2,128)(2,1)S(1)}, bf16[2,128,1,384]{3,2,1,0:T(2,128)(2,1)}, u32[]{:S(2)}) copy-start(bf16[2,128,1,384]{3,2,1,0:T(2,128)(2,1)} %copy-done.10) | copy-start | bytes 589828
  106.4 90.8 %reduce-scatter.5.cloned.1.call-start = ((), (), s32[]{:S(2)}) async-start(), calls=%async_computation.4 | async-start | bytes 1769472 | tf_op jit(solution)/shard_map/reduce_scatter | solution.py:135
  159.4 1.1 copy-start.18
  162.9 0.7 copy-start.56
  162.9 0.7 copy-start.58
  162.9 0.8 copy-start.26
  162.9 0.8 copy-start.48
  162.9 0.8 copy-start.50
  162.9 0.8 copy-start.52
  162.9 0.8 copy-start.54
  162.9 10.7 %copy-start.21 = (f32[4,128,128]{1,2,0:T(8,128)S(1)}, f32[4,128,128]{1,2,0:T(8,128)}, u32[]{:S(2)}) copy-start(f32[4,128,128]{1,2,0:T(8,128)} %get-tuple-element.1487) | copy-start | bytes 786436
  (37 other events, 23.6 us)
Sparse Core Ops, SparseCore 0:
  14.5 29.9 all-gather.1
  68.0 35.1 reduce-scatter.2
  106.9 52.4 all-reduce.2
  163.1 34.0 reduce-scatter.4
where the time goes:
time: 204 us
  waiting for transfers between devices  119 us (58%)
  local copies, waits for them, and re-layouts  24.4 us (12%)
  blocking collectives  19.7 us (10%)
  between operations  17.5 us (9%)
  matrix products  12.4 us (6%)
  other arithmetic  10.2 us (5%)
    psum x1, waiting for transfers between devices, local(): wq_total, wk_total = lax.psum((wq_term, wk_terms), 'ctx')  52.9 us
    reduce_scatter x1, waiting for transfers between devices, local(): lax.psum_scatter(grad_key_all, 'ctx', scatter_dimension=1, tiled=True)  33.1 us
    reduce_scatter x1, waiting for transfers between devices, local(): lax.psum_scatter(whole.reshape(features * kv_heads, gate_dim), 'head', sc...  22.7 us
    all_gather x1, blocking collectives, local(): doc_all = lax.all_gather(doc_ids, 'ctx', axis=1, tiled=True)  11.7 us
    all_gather x1, waiting for transfers between devices, local(): key_all = lax.all_gather(key_local, 'ctx', axis=1, tiled=True)  9.98 us
    unnamed x125, local copies, waits for them, and re-layouts  9.81 us
    all_gather x1, blocking collectives, local(): all_losses = lax.all_gather(losses, 'ctx', axis=2, tiled=True)  8.01 us
    dot_general x8, matrix products, scores_at(): jnp.einsum('sgd,skd->sgk', q_rows, k_tile, preferred_element_type=jnp.flo...  6.38 us
  transfers between devices with their start and end apart: 4, of which 4 were waited for; matrix products, arithmetic and copies ran while one was open for 5% of the time, Pallas kernels for 0%

commit v1 on v0

v1 whole, which is shorter than its diff:
```python
import functools
import math

import jax
import jax.numpy as jnp
from jax import lax
from jax.experimental import pallas as pl
from jax.experimental.pallas import tpu as pltpu
from jax.sharding import PartitionSpec as P

NEG_FILL = -1e30
MESH = pl.DeviceIdType.MESH
F32 = jnp.float32
BF16 = jnp.bfloat16


def dot_nt(a, b):
    return lax.dot_general(a, b, (((1,), (1,)), ((), ())), preferred_element_type=F32)


def dot_tn(a, b):
    return lax.dot_general(a, b, (((0,), (0,)), ((), ())), preferred_element_type=F32)


def dot_nn(a, b):
    return lax.dot_general(a, b, (((1,), (0,)), ((), ())), preferred_element_type=F32)


def kernel(
    dims,
    pq_hbm, pk_hbm, wq_hbm, wk_hbm, t_hbm, doc_ref, own_ref,
    wq_out, wk_out, kl_out,
    pq, pk, wq, wk, tch, kbuf, qg, qrecv, dsend, drecv, gq, gk,
    wq_part, wq_recv, wq_sum, wq_all, wk_part, wk_recv, wk_sum, wk_all, kl_send, kl_all,
    load_sem, k_send, k_recv, q_send, q_recv, d_send, d_recv, l_send, l_recv,
    a_send, a_recv, b_send, b_recv, e_send, e_recv, f_send, f_recv,
):
    C, D, S, R, L, E, F, KVH, group, W, K, FC = dims
    DH = E if pq.shape[2] == L * E else pq.shape[2] // L
    c = lax.axis_index("ctx")
    d = lax.axis_index("head")
    me = c * D + d
    scale = 1.0 / math.sqrt(E)
    share = group // L

    def remote(src, dst, ssem, rsem, cc, dd):
        return pltpu.make_async_remote_copy(
            src_ref=src, dst_ref=dst, send_sem=ssem, recv_sem=rsem,
            device_id=(cc, dd), device_id_type=MESH,
        )

    barrier = pltpu.get_barrier_semaphore()

    def greet(i, carry):
        @pl.when(i != me)
        def _():
            pl.semaphore_signal(barrier, inc=1, device_id=(i // D, i % D), device_id_type=MESH)
        return carry

    lax.fori_loop(0, C * D, greet, 0)

    g = (d * L) // group
    loads = [
        pltpu.make_async_copy(pk_hbm, pk, load_sem.at[0]),
        pltpu.make_async_copy(wk_hbm.at[g], wk, load_sem.at[1]),
        pltpu.make_async_copy(pq_hbm, pq, load_sem.at[2]),
        pltpu.make_async_copy(wq_hbm, wq, load_sem.at[3]),
    ]
    for k in range(W):
        col = pl.multiple_of(jnp.maximum(c - k, 0) * R, R)
        loads.append(
            pltpu.make_async_copy(t_hbm.at[:, :, :, pl.ds(col, R)], tch.at[k], load_sem.at[4 + k])
        )
    for load in loads:
        load.start()

    loads[0].wait()
    loads[1].wait()
    docs = doc_ref[...].astype(F32)
    for s in range(S):
        kbuf[0, s, 0:R, :] = dot_nn(pk[s], wk[...]).astype(BF16)
        kbuf[0, s, R : R + 16, :] = jnp.broadcast_to(docs[s : s + 1, :], (16, R)).astype(BF16)
    loads[2].wait()
    loads[3].wait()
    for s in range(S):
        for h in range(L):
            qg[s, h] = dot_nn(pq[s, :, h * DH : (h + 1) * DH], wq[h]).astype(BF16)
    for k in range(1, W):
        @pl.when(c < k)
        def _(k=k):
            kbuf[k] = jnp.zeros(kbuf.shape[1:], BF16)

        @pl.when(c + k >= C)
        def _(k=k):
            qrecv[k - 1] = jnp.zeros(qrecv.shape[1:], BF16)
            drecv[k - 1] = jnp.zeros(drecv.shape[1:], BF16)

    pl.semaphore_wait(barrier, C * D - 1)

    def key_copy(k):
        return remote(kbuf.at[0], kbuf.at[k], k_send.at[k - 1], k_recv.at[k - 1], c + k, d)

    def query_copy(k):
        return remote(qg, qrecv.at[k - 1], q_send.at[k - 1], q_recv.at[k - 1], c - k, d)

    def diff_copy(k, s, h):
        return remote(
            dsend.at[k, s, h], drecv.at[k - 1, s, h],
            d_send.at[k - 1, s, h], d_recv.at[k - 1, s, h], c - k, d,
        )

    for k in range(1, W):
        @pl.when(c + k < C)
        def _(k=k):
            key_copy(k).start()
    for k in range(1, W):
        @pl.when(c >= k)
        def _(k=k):
            query_copy(k).start()
    for load in loads[4:]:
        load.wait()
    for k in range(1, W):
        @pl.when(c >= k)
        def _(k=k):
            key_copy(k).wait_recv()

    rows_i = lax.broadcasted_iota(jnp.int32, (R, R), 0)
    cols_i = lax.broadcasted_iota(jnp.int32, (R, R), 1)
    causal = rows_i >= cols_i
    lane = lax.broadcasted_iota(jnp.int32, (R, 128), 1)
    kl_cols = jnp.zeros((R, 128), F32)

    def send_diff(s, h):
        for k in range(1, W):
            @pl.when(c >= k)
            def _(k=k):
                diff_copy(k, s, h).start()

    pending = None
    for s in range(S):
        row_doc = jnp.transpose(jnp.broadcast_to(docs[s : s + 1, :], (R, R)))
        allowed = []
        for k in range(W):
            col_doc = kbuf[k, s, R : R + 16, :].astype(F32)[0:1, :]
            same = row_doc == jnp.broadcast_to(col_doc, (R, R))
            allowed.append(same & (causal if k == 0 else (rows_i >= jnp.where(c >= k, 0, R))))
        for h in range(L):
            q = qg[s, h]
            raws = [dot_nt(q, kbuf[k, s, 0:R, :]) * scale for k in range(W)]
            tops = [jnp.where(allowed[k], raws[k], NEG_FILL) for k in range(W)]
            top = jnp.max(functools.reduce(jnp.maximum, tops), axis=1, keepdims=True)
            expos, tms = [], []
            total = mass = entropy = cross = 0.0
            for k in range(W):
                shifted = jnp.where(allowed[k], raws[k] - top, 0.0)
                expo = jnp.where(allowed[k], jnp.exp(shifted), 0.0)
                t = tch[k, s, h].astype(F32)
                tm = jnp.where(allowed[k], t, 0.0)
                expos.append(expo)
                tms.append(tm)
                total = total + expo
                mass = mass + tm
                entropy = entropy + tm * jnp.log(t)
                cross = cross + tm * shifted
            total = jnp.sum(total, axis=1, keepdims=True)
            mass = jnp.sum(mass, axis=1, keepdims=True)
            inner = jnp.sum(entropy - cross, axis=1, keepdims=True)
            kl = inner / mass - jnp.log(mass) + jnp.log(total)
            kl_cols = jnp.where(lane == s * L + h, kl, kl_cols)
            inv_total = 1.0 / total
            inv_mass = 1.0 / mass
            grad = 0.0
            for k in range(W):
                diff = (expos[k] * inv_total - tms[k] * inv_mass).astype(BF16)
                dsend[k, s, h] = diff
                grad = grad + dot_nn(diff, kbuf[k, s, 0:R, :])
            gq[h, s * R : (s + 1) * R, :] = (scale * grad).astype(BF16)
            if pending is not None:
                send_diff(*pending)
            pending = (s, h)

    kl_send[...] = jnp.transpose(kl_cols)[0 : S * L, :]
    for h in range(L):
        left = jnp.concatenate([pq[s, :, h * DH : (h + 1) * DH] for s in range(S)], axis=0)
        term = dot_tn(left, gq[h])
        step = wq_part.shape[1]
        for i in range(DH // step if step < DH else 1):
            slot = (h * DH) // step + i
            at = (h * DH) % step
            size = min(step, DH)
            wq_part[slot, at : at + size, :] = term[i * size : (i + 1) * size, :]
    send_diff(*pending)

    def others(fn):
        for o in range(1, C):
            fn(o, lax.rem(c + o, C), lax.rem(c + C - o, C))

    def a_copy(o, to):
        return remote(wq_part.at[to], wq_recv.at[o - 1], a_send.at[o - 1], a_recv.at[o - 1], to, d)

    def l_copy(o, to):
        return remote(kl_send, kl_all.at[c], l_send.at[o - 1], l_recv.at[o - 1], to, d)

    def b_copy(o, to):
        return remote(wq_sum, wq_all.at[c], b_send.at[o - 1], b_recv.at[o - 1], to, d)

    def f_copy(o, to):
        return remote(wk_sum, wk_all.at[c], f_send.at[o - 1], f_recv.at[o - 1], to, d)

    others(lambda o, to, fr: a_copy(o, to).start())
    others(lambda o, to, fr: l_copy(o, to).start())

    for k in range(1, W):
        @pl.when(c + k < C)
        def _(k=k):
            remote(
                qg, qrecv.at[k - 1], q_send.at[k - 1], q_recv.at[k - 1], c + k, d
            ).wait_recv()

    for s in range(S):
        for h in range(L):
            total = dot_tn(dsend[0, s, h], qg[s, h])
            for k in range(1, W):
                @pl.when(c + k < C)
                def _(k=k, s=s, h=h):
                    remote(
                        dsend.at[k, s, h], drecv.at[k - 1, s, h],
                        d_send.at[k - 1, s, h], d_recv.at[k - 1, s, h], c + k, d,
                    ).wait_recv()
                total = total + dot_tn(drecv[k - 1, s, h], qrecv[k - 1, s, h])
            gk[s * R : (s + 1) * R, h * E : (h + 1) * E] = (scale * total).astype(BF16)

    left = jnp.concatenate([pk[s] for s in range(S)], axis=0)
    wide = dot_tn(left, gk[...])
    term = wide[:, 0:E]
    for h in range(1, L):
        term = term + wide[:, h * E : (h + 1) * E]
    for i in range(D * K):
        wk_part[i // K, i % K] = term[i * FC : (i + 1) * FC, :]

    own = wq_part[c]
    for o in range(1, C):
        a_copy(o, lax.rem(c + o, C)).wait_recv()
        own = own + wq_recv[o - 1]
    wq_sum[...] = own

    def e_copy(i):
        return remote(
            wk_part.at[i // K % D, i % K], wk_recv.at[c, d],
            e_send.at[i], e_recv.at[c, d], i % K, i // K,
        )

    def scatter(i, carry):
        @pl.when((i % K) * D + i // K != me)
        def _():
            e_copy(i).start()
        return carry

    lax.fori_loop(0, D * K, scatter, 0)
    others(lambda o, to, fr: b_copy(o, to).start())

    wq_all[c] = own

    others(lambda o, to, fr: l_copy(o, fr).wait_recv())
    kl_all[c] = kl_send[...]
    owner = own_ref[...]
    picked = jnp.zeros((S * L, R), F32)
    for cc in range(C):
        hot = (rows_i + cc * R == jnp.broadcast_to(owner, (R, R))).astype(F32)
        picked = picked + lax.dot_general(
            kl_all[cc], hot, (((1,), (0,)), ((), ())),
            precision=lax.Precision.HIGHEST, preferred_element_type=F32,
        )
    for s in range(S):
        kl_out[s] = picked[s * L : (s + 1) * L, :]

    @pl.when(c < K)
    def _():
        wk_recv[c, d] = wk_part[d, c % K]

        def arrive(i, carry):
            cc, dd = i // D, i % D

            @pl.when(i != me)
            def _():
                remote(
                    wk_part.at[0, 0], wk_recv.at[cc, dd],
                    e_send.at[0], e_recv.at[cc, dd], cc, dd,
                ).wait_recv()
            return carry

        lax.fori_loop(0, C * D, arrive, 0)
        for kv in range(KVH):
            acc = None
            for cc in range(C):
                for dd in range(kv * share, (kv + 1) * share):
                    piece = wk_recv[cc, dd]
                    acc = piece if acc is None else acc + piece
            wk_sum[:, kv, :] = acc
        others(lambda o, to, fr: f_copy(o, to).start())
        wk_all[c] = wk_sum[...]

    others(lambda o, to, fr: b_copy(o, to).wait_recv())
    wq_out[...] = wq_all[...]

    for o in range(1, C):
        @pl.when(lax.rem(c + C - o, C) < K)
        def _(o=o):
            f_copy(o, lax.rem(c + o, C)).wait_recv()
    wk_out[...] = wk_all[0:K]

    for k in range(1, W):
        @pl.when(c + k < C)
        def _(k=k):
            key_copy(k).wait_send()

        @pl.when(c >= k)
        def _(k=k):
            query_copy(k).wait_send()
            for s in range(S):
                for h in range(L):
                    diff_copy(k, s, h).wait_send()
    others(lambda o, to, fr: a_copy(o, to).wait_send())
    others(lambda o, to, fr: l_copy(o, to).wait_send())
    others(lambda o, to, fr: b_copy(o, to).wait_send())

    @pl.when(c < K)
    def _():
        others(lambda o, to, fr: f_copy(o, to).wait_send())

    def gone(i, carry):
        @pl.when((i % K) * D + i // K != me)
        def _():
            e_copy(i).wait_send()
        return carry

    lax.fori_loop(0, D * K, gone, 0)


def local(C, D, pooled_q, pooled_k, wq, wk, teacher, doc_ids, owner_rows):
    S, R, width = pooled_q.shape
    L, DH, E = wq.shape
    KVH, F, unused = wk.shape
    group = D * L // KVH
    blocks = teacher.shape[3]
    longest = blocks // 2
    W = min(C, (longest - 2) // R + 2)
    FL = F // D
    K = math.gcd(C, FL)
    FC = FL // K
    CH = L * DH // C
    dims = (C, D, S, R, L, E, F, KVH, group, W, K, FC)
    kv = (lax.axis_index("head") * L) // group
    pk = lax.dynamic_index_in_dim(pooled_k, kv, 2, keepdims=False)
    V = pltpu.VMEM
    dma = pltpu.SemaphoreType.DMA
    any_spec = pl.BlockSpec(memory_space=pl.ANY)
    vmem = pl.BlockSpec(memory_space=pltpu.VMEM)
    n = max(C - 1, 1)
    wq_total, wk_grad, row_kl = pl.pallas_call(
        functools.partial(kernel, dims),
        out_shape=(
            jax.ShapeDtypeStruct((C, CH, E), F32),
            jax.ShapeDtypeStruct((K, FC, KVH, E), F32),
            jax.ShapeDtypeStruct((S, L, R), F32),
        ),
        in_specs=[any_spec] * 5 + [vmem, vmem],
        out_specs=(vmem, vmem, vmem),
        scratch_shapes=[
            V((S, R, width), BF16), V((S, R, F), BF16), V((L, DH, E), BF16), V((F, E), BF16),
            V((W, S, L, R, R), BF16), V((W, S, R + 16, E), BF16), V((S, L, R, E), BF16),
            V((W - 1, S, L, R, E), BF16), V((W, S, L, R, R), BF16), V((W - 1, S, L, R, R), BF16),
            V((L, S * R, E), BF16), V((S * R, L * E), BF16),
            V((C, CH, E), F32), V((n, CH, E), F32), V((CH, E), F32), V((C, CH, E), F32),
            V((D, K, FC, E), F32), V((C, D, FC, E), F32), V((FC, KVH, E), F32),
            V((C, FC, KVH, E), F32), V((S * L, R), F32), V((C, S * L, R), F32),
            dma((4 + W,)), dma((W - 1,)), dma((W - 1,)), dma((W - 1,)), dma((W - 1,)),
            dma((W - 1, S, L)), dma((W - 1, S, L)), dma((n,)), dma((n,)),
            dma((n,)), dma((n,)), dma((n,)), dma((n,)), dma((D * K,)), dma((C, D)),
            dma((n,)), dma((n,)),
        ],
        compiler_params=pltpu.CompilerParams(collective_id=0, has_side_effects=True),
    )(pooled_q, pk, wq, wk, teacher, doc_ids, owner_rows.reshape(1, R))
    return (
        wq_total.reshape(L, DH, E),
        wk_grad.reshape(K * FC * KVH, E),
        row_kl,
    )


def solution(mesh):
    placed = (
        P(None, "ctx", "head"),
        P(None, "ctx", None, None),
        P("head", None, None),
        P(),
        P(None, "head", "ctx", None),
        P(None, "ctx"),
        P("ctx"),
    )
    return jax.shard_map(
        functools.partial(local, mesh.shape["ctx"], mesh.shape["head"]),
        mesh=mesh,
        in_specs=placed,
        out_specs=(P("head", None, None), P("head", None), P(None, "head", "ctx")),
        check_vma=False,
    )
```

time: 204 us -> 57.2 us (0.28)
  waiting for transfers between devices: 119 us -> 0 us
  Pallas kernels: 0 us -> 49.2 us
  blocking collectives: 19.7 us -> 0 us
  local copies, waits for them, and re-layouts: 24.4 us -> 7.06 us
  between operations: 17.5 us -> 0.67 us
  matrix products: 12.4 us -> 0 us
  other arithmetic: 10.2 us -> 0 us
    reduce_scatter x2 -> x0, waiting for transfers between devices: 55.8 us -> none  [the longest x1 33.1 us: local(): lax.psum_scatter(grad_key_all, 'ctx', scatter_dimension=1, tiled=True)]
    psum x1 -> x0, waiting for transfers between devices: 52.9 us -> none  [local(): wq_total, wk_total = lax.psum((wq_term, wk_terms), 'ctx')]
    pallas_call x0 -> x1, Pallas kernels: none -> 49.2 us  [local(): pl.pallas_call(functools.partial(kernel, dims), out_shape=(jax.ShapeDtype...]
    all_gather x2 -> x0, blocking collectives: 19.7 us -> none  [the longest x1 11.7 us: local(): doc_all = lax.all_gather(doc_ids, 'ctx', axis=1, tiled=True)]
    dot_general x26 -> x0, matrix products: 12.4 us -> none  [the longest x8 6.38 us: scores_at(): jnp.einsum('sgd,skd->sgk', q_rows, k_tile, preferred_element_type=jnp.flo...]
    all_gather x1 -> x0, waiting for transfers between devices: 9.98 us -> none  [local(): key_all = lax.all_gather(key_local, 'ctx', axis=1, tiled=True)]
    dynamic_slice x1, local copies, waits for them, and re-layouts: 5.17 us -> 0.41 us  [local(): pk = lax.dynamic_index_in_dim(pooled_k, kv, 2, keepdims=False)]
    reduce_sum x4 -> x0, other arithmetic: 3.5 us -> none  [first_pass(): cross = cross + jnp.sum(jnp.where(allowed, tch * raw, 0.0), axis=2)]
  transfers between devices with their start and end apart: 4 -> 0, of which waited for: 4 -> 0; matrix products, arithmetic and copies ran while one was open for 5% -> 0% of each run, Pallas kernels for 0% -> 0%
where the time goes in v1:
time: 57.2 us; the launch traced here: 57 us
  Pallas kernels  49.2 us (86%)
  local copies, waits for them, and re-layouts  7.06 us (12%)
  between operations  0.67 us (1%)
    pallas_call x1, Pallas kernels, local(): pl.pallas_call(functools.partial(kernel, dims), out_shape=(jax.ShapeDtype...  49.2 us
    unnamed x6, local copies, waits for them, and re-layouts  6.65 us

profile of v1, /device:TPU:0, one launch (start us, length us, event | category | flops | bytes accessed | tf_op | source)
XLA Modules:
  0.0 57.0 jit_solution(16858756596118256033)
XLA Ops:
  0.6 0.0 copy-start
  0.7 1.4 %copy-done = bf16[2,128,8,384]{3,2,1,0:T(8,128)(2,1)S(1)} copy-done((bf16[2,128,8,384]{3,2,1,0:T(8,128)(2,1)S(1)}, bf16[2,128,8,384]{3,2,1,0:T(8,128)(2,1)}, u32[]{:S(2)}) %copy-start) | copy-done | bytes 1572888
  2.0 0.4 constant_dynamic-slice_fusion
  2.5 0.7 %copy.13 = bf16[2,128,1,384]{3,1,0,2:T(8,128)(2,1)} copy(bf16[2,128,1,384]{3,2,1,0:T(2,128)(2,1)S(1)} %constant_dynamic-slice_fusion) | data formatting | bytes 393216
  3.2 49.2 %shard_map.94 = (f32[4,128,128]{2,1,0:T(8,128)}, f32[4,12,8,128]{3,2,1,0:T(8,128)}, f32[2,4,128]{2,1,0:T(4,128)}) custom-call(bf16[2,128,512]{2,1,0:T(8,128)(2,1)} %pq_hbm.1, bf16[2,128,384]{2,1,0:T(8,128)(2,1)} %bitcast.5, bf16[4,128,128]{2,1,0:T(8,128)(2,1)} %wq_hbm.1, bf16[8,384,128]{2,1,0:T(8,128)(2,1)} %wk_hbm.1, bf16[2,4,128,512]{3,2,1,0:T(8,128)(2,1)} %t_hbm.1, ...), custom_call_target="tpu_custom_call" | custom-call | tf_op jit(solution)/shard_map/pallas_call | solution.py:360
  52.4 1.7 %copy.17 = f32[4,128,128]{2,1,0:T(8,128)} copy(f32[4,128,128]{2,1,0:T(8,128)} %get-tuple-element.12) | data formatting | bytes 524288
  54.1 1.6 %copy.18 = f32[384,128]{1,0:T(8,128)} copy(f32[384,128]{1,0:T(8,128)} %bitcast.6) | data formatting | bytes 393216
  55.7 1.3 %copy.19 = f32[2,4,128]{2,1,0:T(4,128)} copy(f32[2,4,128]{2,1,0:T(4,128)} %get-tuple-element.14) | data formatting | bytes 8192
Async XLA Ops:
  0.6 1.4 %copy-start = (bf16[2,128,8,384]{3,2,1,0:T(8,128)(2,1)S(1)}, bf16[2,128,8,384]{3,2,1,0:T(8,128)(2,1)}, u32[]{:S(2)}) copy-start(bf16[2,128,8,384]{3,2,1,0:T(8,128)(2,1)} %param.8) | copy-start | bytes 4718596

commit v2 on v1

v2 whole, which is shorter than its diff:
```python
import functools
import math

import jax
import jax.numpy as jnp
from jax import lax
from jax.experimental import pallas as pl
from jax.experimental.pallas import tpu as pltpu
from jax.sharding import PartitionSpec as P

NEG_FILL = -1e30
MESH = pl.DeviceIdType.MESH
F32 = jnp.float32
BF16 = jnp.bfloat16


def dot_nt(a, b):
    return lax.dot_general(a, b, (((1,), (1,)), ((), ())), preferred_element_type=F32)


def dot_tn(a, b):
    return lax.dot_general(a, b, (((0,), (0,)), ((), ())), preferred_element_type=F32)


def dot_nn(a, b):
    return lax.dot_general(a, b, (((1,), (0,)), ((), ())), preferred_element_type=F32)


def plan(C, S, W):
    side = math.isqrt(C)
    own = [[j for j in range(C)] for s in range(S)]
    if side * side != C or side != 2:
        return own
    for s in range(0, S, 2):
        own[s][side - 1] = C - 1
    return own


def kernel(
    dims, own,
    pq_hbm, pk_hbm, wq_hbm, wk_hbm, t_hbm, doc_ref, own_ref,
    wq_out, wk_out, kl_out,
    pq, pkall, pkb, wq, wk, tch, kbuf, qbuf, dbuf, gq, gk, acc, term,
    wq_part, wq_recv, wq_sum, wq_all, wk_part, wk_recv, wk_sum, wk_all, kl_send, kl_all,
    load_sem, k_send, k_recv, q_send, q_recv, p_send, p_recv, d_send, d_recv, l_send, l_recv,
    a_send, a_recv, b_send, b_recv, e_send, e_recv, f_send, f_recv,
):
    C, D, S, R, L, E, F, KVH, group, W, K, FC = dims
    DH = wq.shape[1]
    c = lax.axis_index("ctx")
    d = lax.axis_index("head")
    me = c * D + d
    scale = 1.0 / math.sqrt(E)
    share = group // L

    def remote(src, dst, ssem, rsem, cc, dd):
        return pltpu.make_async_remote_copy(
            src_ref=src, dst_ref=dst, send_sem=ssem, recv_sem=rsem,
            device_id=(cc, dd), device_id_type=MESH,
        )

    def pick(values):
        out = jnp.int32(values[0])
        for cc in range(1, C):
            out = jnp.where(c == cc, jnp.int32(values[cc]), out)
        return out

    diff_to = [[[own[s][cc - k] if cc >= k else cc for cc in range(C)] for k in range(W)] for s in range(S)]
    query_to = []
    for s in range(S):
        lists = [sorted({diff_to[s][k][cc] for k in range(W)} - {cc}) for cc in range(C)]
        most = max(len(item) for item in lists)
        query_to.append([[item[t] if t < len(item) else cc for cc, item in enumerate(lists)] for t in range(most)])
    query_from = [
        [[int(any(t[src] == cc for t in query_to[s]) and src != cc) for cc in range(C)] for src in range(C)]
        for s in range(S)
    ]
    owned = []
    for s in range(S):
        lists = [[j for j in range(C) if own[s][j] == cc] for cc in range(C)]
        most = max(len(item) for item in lists)
        owned.append([[item[e] if e < len(item) else -1 for item in lists] for e in range(most)])
    key_to = [[own[s][cc] for cc in range(C)] for s in range(S)]

    barrier = pltpu.get_barrier_semaphore()

    def greet(i, carry):
        @pl.when(i != me)
        def _():
            pl.semaphore_signal(barrier, inc=1, device_id=(i // D, i % D), device_id_type=MESH)
        return carry

    g = (d * L) // group
    loads = [
        pltpu.make_async_copy(pk_hbm, pkall, load_sem.at[0]),
        pltpu.make_async_copy(wk_hbm.at[g], wk, load_sem.at[1]),
        pltpu.make_async_copy(pq_hbm, pq, load_sem.at[2]),
        pltpu.make_async_copy(wq_hbm, wq, load_sem.at[3]),
    ]
    for k in range(W):
        col = pl.multiple_of(jnp.maximum(c - k, 0) * R, R)
        loads.append(
            pltpu.make_async_copy(t_hbm.at[:, :, :, pl.ds(col, R)], tch.at[k], load_sem.at[4 + k])
        )
    for load in loads:
        load.start()
    lax.fori_loop(0, C * D, greet, 0)

    loads[0].wait()
    loads[1].wait()
    docs = doc_ref[...].astype(F32)
    wide_r = lax.broadcasted_iota(jnp.int32, (R, R * KVH), 0)
    wide_c = lax.broadcasted_iota(jnp.int32, (R, R * KVH), 1)
    choose = (wide_c == wide_r * KVH + g).astype(F32).astype(BF16)
    for s in range(S):
        feats = dot_nn(choose, pkall[s]).astype(BF16)
        pkb[c, s] = feats
        kbuf[c, s, 0:R, :] = dot_nn(feats, wk[...]).astype(BF16)
        kbuf[c, s, R : R + 16, :] = jnp.broadcast_to(docs[s : s + 1, :], (16, R)).astype(BF16)
    loads[2].wait()
    loads[3].wait()
    for s in range(S):
        for h in range(L):
            qbuf[c, s, h] = dot_nn(pq[s, :, h * DH : (h + 1) * DH], wq[h]).astype(BF16)

    pl.semaphore_wait(barrier, C * D - 1)

    def key_copy(k, src, to):
        return remote(kbuf.at[src], kbuf.at[src], k_send.at[k - 1], k_recv.at[k - 1], to, d)

    def query_copy(s, t, src, to):
        return remote(qbuf.at[src, s], qbuf.at[src, s], q_send.at[t, s], q_recv.at[src, s], to, d)

    def feat_copy(s, src, to):
        return remote(pkb.at[src, s], pkb.at[src, s], p_send.at[s], p_recv.at[src, s], to, d)

    def diff_copy(k, s, h, src, to):
        return remote(
            dbuf.at[src, s, k, h], dbuf.at[src, s, k, h],
            d_send.at[s, k, h], d_recv.at[src, s, k, h], to, d,
        )

    def each_query(fn):
        for s in range(S):
            for t in range(len(query_to[s])):
                to = pick(query_to[s][t])

                @pl.when(to != c)
                def _(s=s, t=t, to=to):
                    fn(query_copy(s, t, c, to))

    def each_feat(fn):
        for s in range(S):
            if any(key_to[s][cc] != cc for cc in range(C)):
                to = pick(key_to[s])

                @pl.when(to != c)
                def _(s=s, to=to):
                    fn(feat_copy(s, c, to))

    def each_diff(s, h, fn):
        for k in range(W):
            if any(diff_to[s][k][cc] != cc for cc in range(C)):
                to = pick(diff_to[s][k])

                @pl.when(to != c)
                def _(k=k, to=to):
                    fn(diff_copy(k, s, h, c, to))

    for k in range(1, W):
        @pl.when(c + k < C)
        def _(k=k):
            key_copy(k, c, c + k).start()
    each_query(lambda copy: copy.start())
    each_feat(lambda copy: copy.start())
    for load in loads[4:]:
        load.wait()

    rows_i = lax.broadcasted_iota(jnp.int32, (R, R), 0)
    cols_i = lax.broadcasted_iota(jnp.int32, (R, R), 1)
    causal = rows_i >= cols_i
    lane = lax.broadcasted_iota(jnp.int32, (R, 128), 1)
    kl_cols = jnp.zeros((R, 128), F32)
    at = [c] + [jnp.maximum(c - k, 0) for k in range(1, W)]

    for k in range(1, W):
        @pl.when(c >= k)
        def _(k=k):
            key_copy(k, c - k, c).wait_recv()

    pending = None
    for s in range(S):
        row_doc = jnp.transpose(jnp.broadcast_to(docs[s : s + 1, :], (R, R)))
        allowed = []
        for k in range(W):
            col_doc = kbuf[at[k], s, R : R + 16, :].astype(F32)[0:1, :]
            same = row_doc == jnp.broadcast_to(col_doc, (R, R))
            allowed.append(same & (causal if k == 0 else (rows_i >= jnp.where(c >= k, 0, R))))
        for h in range(L):
            q = qbuf[c, s, h]
            raws = [dot_nt(q, kbuf[at[k], s, 0:R, :]) * scale for k in range(W)]
            tops = [jnp.where(allowed[k], raws[k], NEG_FILL) for k in range(W)]
            top = jnp.max(functools.reduce(jnp.maximum, tops), axis=1, keepdims=True)
            expos, tms = [], []
            total = mass = inner = 0.0
            for k in range(W):
                shifted = jnp.where(allowed[k], raws[k] - top, 0.0)
                expo = jnp.where(allowed[k], jnp.exp(shifted), 0.0)
                t = tch[k, s, h].astype(F32)
                tm = jnp.where(allowed[k], t, 0.0)
                expos.append(expo)
                tms.append(tm)
                total = total + expo
                mass = mass + tm
                inner = inner + tm * (jnp.log(t) - shifted)
            total = jnp.sum(total, axis=1, keepdims=True)
            mass = jnp.sum(mass, axis=1, keepdims=True)
            inner = jnp.sum(inner, axis=1, keepdims=True)
            kl = inner / mass - jnp.log(mass) + jnp.log(total)
            kl_cols = jnp.where(lane == s * L + h, kl, kl_cols)
            inv_total = 1.0 / total
            inv_mass = 1.0 / mass
            grad = 0.0
            for k in range(W):
                diff = (expos[k] * inv_total - tms[k] * inv_mass).astype(BF16)
                dbuf[c, s, k, h] = diff
                grad = grad + dot_nn(diff, kbuf[at[k], s, 0:R, :])
            gq[h, s * R : (s + 1) * R, :] = (scale * grad).astype(BF16)
            if pending is not None:
                each_diff(*pending, lambda copy: copy.start())
            pending = (s, h)

    kl_send[...] = jnp.transpose(kl_cols)[0 : S * L, :]
    for h in range(L):
        left = jnp.concatenate([pq[s, :, h * DH : (h + 1) * DH] for s in range(S)], axis=0)
        part = dot_tn(left, gq[h])
        step = wq_part.shape[1]
        size = min(step, DH)
        for i in range(DH // size):
            slot = (h * DH + i * size) // step
            off = (h * DH + i * size) % step
            wq_part[slot, off : off + size, :] = part[i * size : (i + 1) * size, :]
    each_diff(*pending, lambda copy: copy.start())

    def others(fn):
        for o in range(1, C):
            fn(o, lax.rem(c + o, C), lax.rem(c + C - o, C))

    def a_copy(o, to):
        return remote(wq_part.at[to], wq_recv.at[o - 1], a_send.at[o - 1], a_recv.at[o - 1], to, d)

    def l_copy(o, to):
        return remote(kl_send, kl_all.at[c], l_send.at[o - 1], l_recv.at[o - 1], to, d)

    def b_copy(o, to):
        return remote(wq_sum, wq_all.at[c], b_send.at[o - 1], b_recv.at[o - 1], to, d)

    def f_copy(o, to):
        return remote(wk_sum, wk_all.at[c], f_send.at[o - 1], f_recv.at[o - 1], to, d)

    others(lambda o, to, fr: a_copy(o, to).start())
    others(lambda o, to, fr: l_copy(o, to).start())

    for s in range(S):
        for src in range(C):
            if any(query_from[s][src]):
                @pl.when(pick(query_from[s][src]) == 1)
                def _(s=s, src=src):
                    query_copy(s, 0, src, c).wait_recv()

    term[...] = jnp.zeros(term.shape, F32)
    for s in range(S):
        for e in range(len(owned[s])):
            j = pick(owned[s][e])

            @pl.when(j >= 0)
            def _(s=s, e=e, j=j):
                for h in range(L):
                    acc[h] = jnp.zeros((R, E), F32)
                    for k in range(W):
                        src = j + k

                        @pl.when(src < C)
                        def _(h=h, k=k, src=src):
                            @pl.when(src != c)
                            def _():
                                diff_copy(k, s, h, src, c).wait_recv()

                            acc[h] += dot_tn(dbuf[src, s, k, h], qbuf[src, s, h])
                    gk[:, h * E : (h + 1) * E] = (scale * acc[h]).astype(BF16)

                @pl.when(j != c)
                def _():
                    feat_copy(s, j, c).wait_recv()

                wide = dot_tn(pkb[j, s], gk[...])
                part = wide[:, 0:E]
                for h in range(1, L):
                    part = part + wide[:, h * E : (h + 1) * E]
                term[...] += part
    for i in range(D * K):
        wk_part[i // K, i % K] = term[i * FC : (i + 1) * FC, :]

    total = wq_part[c]
    for o in range(1, C):
        a_copy(o, lax.rem(c + o, C)).wait_recv()
        total = total + wq_recv[o - 1]
    wq_sum[...] = total

    def e_copy(i):
        return remote(
            wk_part.at[i // K, i % K], wk_recv.at[c, d],
            e_send.at[i], e_recv.at[c, d], i % K, i // K,
        )

    def scatter(i, carry):
        @pl.when((i % K) * D + i // K != me)
        def _():
            e_copy(i).start()
        return carry

    lax.fori_loop(0, D * K, scatter, 0)
    others(lambda o, to, fr: b_copy(o, to).start())

    wq_all[c] = total

    others(lambda o, to, fr: l_copy(o, fr).wait_recv())
    kl_all[c] = kl_send[...]
    owner = own_ref[...]
    picked = jnp.zeros((S * L, R), F32)
    for cc in range(C):
        hot = (rows_i + cc * R == jnp.broadcast_to(owner, (R, R))).astype(F32)
        picked = picked + lax.dot_general(
            kl_all[cc], hot, (((1,), (0,)), ((), ())),
            precision=lax.Precision.HIGHEST, preferred_element_type=F32,
        )
    for s in range(S):
        kl_out[s] = picked[s * L : (s + 1) * L, :]

    @pl.when(c < K)
    def _():
        wk_recv[c, d] = wk_part[d, c % K]

        def arrive(i, carry):
            cc, dd = i // D, i % D

            @pl.when(i != me)
            def _():
                remote(
                    wk_part.at[0, 0], wk_recv.at[cc, dd],
                    e_send.at[0], e_recv.at[cc, dd], cc, dd,
                ).wait_recv()
            return carry

        lax.fori_loop(0, C * D, arrive, 0)
        for kv in range(KVH):
            part = None
            for cc in range(C):
                for dd in range(kv * share, (kv + 1) * share):
                    piece = wk_recv[cc, dd]
                    part = piece if part is None else part + piece
            wk_sum[:, kv, :] = part
        others(lambda o, to, fr: f_copy(o, to).start())
        wk_all[c] = wk_sum[...]

    others(lambda o, to, fr: b_copy(o, to).wait_recv())
    wq_out[...] = wq_all[...]

    for o in range(1, C):
        @pl.when(lax.rem(c + C - o, C) < K)
        def _(o=o):
            f_copy(o, lax.rem(c + o, C)).wait_recv()
    wk_out[...] = wk_all[0:K]

    for k in range(1, W):
        @pl.when(c + k < C)
        def _(k=k):
            key_copy(k, c, c + k).wait_send()
    each_query(lambda copy: copy.wait_send())
    each_feat(lambda copy: copy.wait_send())
    for s in range(S):
        for h in range(L):
            each_diff(s, h, lambda copy: copy.wait_send())
    others(lambda o, to, fr: a_copy(o, to).wait_send())
    others(lambda o, to, fr: l_copy(o, to).wait_send())
    others(lambda o, to, fr: b_copy(o, to).wait_send())

    @pl.when(c < K)
    def _():
        others(lambda o, to, fr: f_copy(o, to).wait_send())

    def gone(i, carry):
        @pl.when((i % K) * D + i // K != me)
        def _():
            e_copy(i).wait_send()
        return carry

    lax.fori_loop(0, D * K, gone, 0)


def finish(a_ref, b_ref, c_ref, x_ref, y_ref, z_ref):
    x_ref[...] = a_ref[...]
    y_ref[...] = b_ref[...]
    z_ref[...] = c_ref[...]


def local(C, D, pooled_q, pooled_k, wq, wk, teacher, doc_ids, owner_rows):
    S, R, width = pooled_q.shape
    L, DH, E = wq.shape
    KVH, F, unused = wk.shape
    group = D * L // KVH
    blocks = teacher.shape[3]
    longest = blocks // 2
    W = min(C, (longest - 2) // R + 2)
    FL = F // D
    K = math.gcd(C, FL)
    FC = FL // K
    CH = L * DH // C
    dims = (C, D, S, R, L, E, F, KVH, group, W, K, FC)
    V = pltpu.VMEM
    dma = pltpu.SemaphoreType.DMA
    any_spec = pl.BlockSpec(memory_space=pl.ANY)
    vmem = pl.BlockSpec(memory_space=pltpu.VMEM)
    n = max(C - 1, 1)
    outs = (
        jax.ShapeDtypeStruct((C, CH, E), F32),
        jax.ShapeDtypeStruct((K, FC, KVH, E), F32),
        jax.ShapeDtypeStruct((S, L, R), F32),
    )
    results = pl.pallas_call(
        functools.partial(kernel, dims, plan(C, S, W)),
        out_shape=outs,
        in_specs=[any_spec] * 5 + [vmem, vmem],
        out_specs=(vmem, vmem, vmem),
        scratch_shapes=[
            V((S, R, width), BF16), V((S, R * KVH, F), BF16), V((C, S, R, F), BF16),
            V((L, DH, E), BF16), V((F, E), BF16),
            V((W, S, L, R, R), BF16), V((C, S, R + 16, E), BF16), V((C, S, L, R, E), BF16),
            V((C, S, W, L, R, R), BF16),
            V((L, S * R, E), BF16), V((R, L * E), BF16), V((L, R, E), F32), V((F, E), F32),
            V((C, CH, E), F32), V((n, CH, E), F32), V((CH, E), F32), V((C, CH, E), F32),
            V((D, K, FC, E), F32), V((C, D, FC, E), F32), V((FC, KVH, E), F32),
            V((C, FC, KVH, E), F32), V((S * L, R), F32), V((C, S * L, R), F32),
            dma((4 + W,)), dma((W - 1,)), dma((W - 1,)), dma((W, S)), dma((C, S)),
            dma((S,)), dma((C, S)),
            dma((S, W, L)), dma((C, S, W, L)), dma((n,)), dma((n,)),
            dma((n,)), dma((n,)), dma((n,)), dma((n,)), dma((D * K,)), dma((C, D)),
            dma((n,)), dma((n,)),
        ],
        compiler_params=pltpu.CompilerParams(collective_id=0, has_side_effects=True),
    )(
        pooled_q, pooled_k.reshape(S, R * KVH, F), wq, wk, teacher, doc_ids,
        owner_rows.reshape(1, R),
    )
    wq_total, wk_grad, row_kl = pl.pallas_call(
        finish, out_shape=outs, in_specs=[vmem] * 3, out_specs=(vmem,) * 3,
    )(*results)
    return (
        wq_total.reshape(L, DH, E),
        wk_grad.reshape(K * FC * KVH, E),
        row_kl,
    )


def solution(mesh):
    placed = (
        P(None, "ctx", "head"),
        P(None, "ctx", None, None),
        P("head", None, None),
        P(),
        P(None, "head", "ctx", None),
        P(None, "ctx"),
        P("ctx"),
    )
    return jax.shard_map(
        functools.partial(local, mesh.shape["ctx"], mesh.shape["head"]),
        mesh=mesh,
        in_specs=placed,
        out_specs=(P("head", None, None), P("head", None), P(None, "head", "ctx")),
        check_vma=False,
    )
```

time: 57.2 us -> 40.6 us (0.71)
  Pallas kernels: 49.2 us -> 39.8 us
  local copies, waits for them, and re-layouts: 7.06 us -> 0 us
    pallas_call x1 -> x2, Pallas kernels: 49.2 us -> 39.8 us  [the longest x1 37.9 us: local(): pl.pallas_call(functools.partial(kernel, dims, plan(C, S, W)), out_shape=...]
    unnamed x6 -> x0, local copies, waits for them, and re-layouts: 6.65 us -> none
where the time goes in v2:
time: 40.6 us; the launch traced here: 40.4 us
  Pallas kernels  39.8 us (98%)
  between operations  0.64 us (2%)
    pallas_call x1, Pallas kernels, local(): pl.pallas_call(functools.partial(kernel, dims, plan(C, S, W)), out_shape=...  37.9 us
    pallas_call x1, Pallas kernels, local(): pl.pallas_call(finish, out_shape=outs, in_specs=[vmem] * 3, out_specs=(vm...  1.84 us

profile of v2, /device:TPU:0, one launch (start us, length us, event | category | flops | bytes accessed | tf_op | source)
XLA Modules:
  0.0 40.4 jit_solution(8489272831200254667)
XLA Ops:
  0.6 37.9 %shard_map.94 = (f32[4,128,128]{2,1,0:T(8,128)}, f32[4,12,8,128]{3,2,1,0:T(8,128)}, f32[2,4,128]{2,1,0:T(4,128)}) custom-call(bf16[2,128,512]{2,1,0:T(8,128)(2,1)} %pq_hbm.1, bf16[2,1024,384]{2,1,0:T(8,128)(2,1)} %bitcast.3, bf16[4,128,128]{2,1,0:T(8,128)(2,1)} %wq_hbm.1, bf16[8,384,128]{2,1,0:T(8,128)(2,1)} %wk_hbm.1, bf16[2,4,128,512]{3,2,1,0:T(8,128)(2,1)} %t_hbm.1, ...), custom_call_target="tpu_custom_call" | custom-call | tf_op jit(solution)/shard_map/pallas_call | solution.py:430
  38.6 1.8 %shard_map.95 = (f32[4,128,128]{2,1,0:T(8,128)}, f32[4,12,8,128]{3,2,1,0:T(8,128)}, f32[2,4,128]{2,1,0:T(4,128)}) custom-call(f32[4,128,128]{2,1,0:T(8,128)} %get-tuple-element.9.a_ref, f32[4,12,8,128]{3,2,1,0:T(8,128)} %get-tuple-element.10.b_ref, f32[2,4,128]{2,1,0:T(4,128)} %get-tuple-element.11.c_ref), custom_call_target="tpu_custom_call" | custom-call | tf_op jit(solution)/shard_map/pallas_call | solution.py:455

commit v3 on v2

--- a/solution.py
+++ b/solution.py
@@ -49,7 +49,6 @@
     DH = wq.shape[1]
     c = lax.axis_index("ctx")
     d = lax.axis_index("head")
-    me = c * D + d
     scale = 1.0 / math.sqrt(E)
     share = group // L
 
@@ -84,11 +83,11 @@
 
     barrier = pltpu.get_barrier_semaphore()
 
-    def greet(i, carry):
-        @pl.when(i != me)
-        def _():
-            pl.semaphore_signal(barrier, inc=1, device_id=(i // D, i % D), device_id_type=MESH)
-        return carry
+    def turn(od):
+        return lax.rem(d + od, D)
+
+    def greet(cc, dd):
+        pl.semaphore_signal(barrier, inc=1, device_id=(cc, dd), device_id_type=MESH)
 
     g = (d * L) // group
     loads = [
@@ -104,7 +103,12 @@
         )
     for load in loads:
         load.start()
-    lax.fori_loop(0, C * D, greet, 0)
+    for od in range(1, D):
+        dd = turn(od)
+        for cc in range(C):
+            greet(cc, dd)
+    for o in range(1, C):
+        greet(lax.rem(c + o, C), d)
 
     loads[0].wait()
     loads[1].wait()
@@ -188,7 +192,7 @@
         def _(k=k):
             key_copy(k, c - k, c).wait_recv()
 
-    pending = None
+    pending = []
     for s in range(S):
         row_doc = jnp.transpose(jnp.broadcast_to(docs[s : s + 1, :], (R, R)))
         allowed = []
@@ -226,9 +230,9 @@
                 dbuf[c, s, k, h] = diff
                 grad = grad + dot_nn(diff, kbuf[at[k], s, 0:R, :])
             gq[h, s * R : (s + 1) * R, :] = (scale * grad).astype(BF16)
-            if pending is not None:
-                each_diff(*pending, lambda copy: copy.start())
-            pending = (s, h)
+            pending.append((s, h))
+            if len(pending) == 2:
+                each_diff(*pending.pop(0), lambda copy: copy.start())
 
     kl_send[...] = jnp.transpose(kl_cols)[0 : S * L, :]
     for h in range(L):
@@ -240,7 +244,8 @@
             slot = (h * DH + i * size) // step
             off = (h * DH + i * size) % step
             wq_part[slot, off : off + size, :] = part[i * size : (i + 1) * size, :]
-    each_diff(*pending, lambda copy: copy.start())
+    for item in pending:
+        each_diff(*item, lambda copy: copy.start())
 
     def others(fn):
         for o in range(1, C):
@@ -275,18 +280,26 @@
 
             @pl.when(j >= 0)
             def _(s=s, e=e, j=j):
+                for k in range(W):
+                    src = j + k
+
+                    @pl.when((src < C) & (src != c))
+                    def _(k=k, src=src):
+                        for h in range(L):
+                            diff_copy(k, s, h, src, c).wait_recv()
+
+                    def product(h, k=k, src=src):
+                        return dot_tn(dbuf[src, s, k, h], qbuf[src, s, h])
+
+                    if k == 0:
+                        for h in range(L):
+                            acc[h] = product(h)
+                    else:
+                        @pl.when(src < C)
+                        def _(product=product):
+                            for h in range(L):
+                                acc[h] += product(h)
                 for h in range(L):
-                    acc[h] = jnp.zeros((R, E), F32)
-                    for k in range(W):
-                        src = j + k
-
-                        @pl.when(src < C)
-                        def _(h=h, k=k, src=src):
-                            @pl.when(src != c)
-                            def _():
-                                diff_copy(k, s, h, src, c).wait_recv()
-
-                            acc[h] += dot_tn(dbuf[src, s, k, h], qbuf[src, s, h])
                     gk[:, h * E : (h + 1) * E] = (scale * acc[h]).astype(BF16)
 
                 @pl.when(j != c)
@@ -301,26 +314,30 @@
     for i in range(D * K):
         wk_part[i // K, i % K] = term[i * FC : (i + 1) * FC, :]
 
+    def e_copy(od, kk):
+        dd = turn(od)
+        return remote(
+            wk_part.at[dd, kk], wk_recv.at[c, d],
+            e_send.at[od * K + kk], e_recv.at[c, d], kk, dd,
+        )
+
+    def each_part(fn):
+        for od in range(1, D):
+            for kk in range(K):
+                fn(e_copy(od, kk))
+        for kk in range(K):
+            @pl.when(kk != c)
+            def _(kk=kk):
+                fn(e_copy(0, kk))
+
+    each_part(lambda copy: copy.start())
+
     total = wq_part[c]
     for o in range(1, C):
         a_copy(o, lax.rem(c + o, C)).wait_recv()
         total = total + wq_recv[o - 1]
     wq_sum[...] = total
 
-    def e_copy(i):
-        return remote(
-            wk_part.at[i // K, i % K], wk_recv.at[c, d],
-            e_send.at[i], e_recv.at[c, d], i % K, i // K,
-        )
-
-    def scatter(i, carry):
-        @pl.when((i % K) * D + i // K != me)
-        def _():
-            e_copy(i).start()
-        return carry
-
-    lax.fori_loop(0, D * K, scatter, 0)
-    others(lambda o, to, fr: b_copy(o, to).start())
 
     wq_all[c] = total
 
@@ -336,23 +353,21 @@
         )
     for s in range(S):
         kl_out[s] = picked[s * L : (s + 1) * L, :]
+    others(lambda o, to, fr: b_copy(o, to).start())
 
     @pl.when(c < K)
     def _():
         wk_recv[c, d] = wk_part[d, c % K]
 
-        def arrive(i, carry):
-            cc, dd = i // D, i % D
-
-            @pl.when(i != me)
-            def _():
-                remote(
-                    wk_part.at[0, 0], wk_recv.at[cc, dd],
-                    e_send.at[0], e_recv.at[cc, dd], cc, dd,
-                ).wait_recv()
-            return carry
-
-        lax.fori_loop(0, C * D, arrive, 0)
+        def came_copy(cc, dd):
+            return remote(wk_part.at[0, 0], wk_recv.at[cc, dd], e_send.at[0], e_recv.at[cc, dd], cc, dd)
+
+        for o in range(1, C):
+            came_copy(lax.rem(c + o, C), d).wait_recv()
+        for od in range(1, D):
+            dd = turn(od)
+            for cc in range(C):
+                came_copy(cc, dd).wait_recv()
         for kv in range(KVH):
             part = None
             for cc in range(C):
@@ -389,13 +404,7 @@
     def _():
         others(lambda o, to, fr: f_copy(o, to).wait_send())
 
-    def gone(i, carry):
-        @pl.when((i % K) * D + i // K != me)
-        def _():
-            e_copy(i).wait_send()
-        return carry
-
-    lax.fori_loop(0, D * K, gone, 0)
+    each_part(lambda copy: copy.wait_send())
 
 
 def finish(a_ref, b_ref, c_ref, x_ref, y_ref, z_ref):

time: 40.6 us -> 39.4 us (0.970)
  Pallas kernels: 39.8 us -> 38.6 us
    pallas_call x1, Pallas kernels: 37.9 us -> 36.8 us  [local(): pl.pallas_call(functools.partial(kernel, dims, plan(C, S, W)), out_shape=...]
where the time goes in v3:
time: 39.4 us; the launch traced here: 39.2 us
  Pallas kernels  38.6 us (98%)
  between operations  0.64 us (2%)
    pallas_call x1, Pallas kernels, local(): pl.pallas_call(functools.partial(kernel, dims, plan(C, S, W)), out_shape=...  36.8 us
    pallas_call x1, Pallas kernels, local(): pl.pallas_call(finish, out_shape=outs, in_specs=[vmem] * 3, out_specs=(vm...  1.84 us

profile of v3, /device:TPU:0, one launch (start us, length us, event | category | flops | bytes accessed | tf_op | source)
XLA Modules:
  0.0 39.2 jit_solution(1312187139537375464)
XLA Ops:
  0.6 36.8 %shard_map.94 = (f32[4,128,128]{2,1,0:T(8,128)}, f32[4,12,8,128]{3,2,1,0:T(8,128)}, f32[2,4,128]{2,1,0:T(4,128)}) custom-call(bf16[2,128,512]{2,1,0:T(8,128)(2,1)} %pq_hbm.1, bf16[2,1024,384]{2,1,0:T(8,128)(2,1)} %bitcast.3, bf16[4,128,128]{2,1,0:T(8,128)(2,1)} %wq_hbm.1, bf16[8,384,128]{2,1,0:T(8,128)(2,1)} %wk_hbm.1, bf16[2,4,128,512]{3,2,1,0:T(8,128)(2,1)} %t_hbm.1, ...), custom_call_target="tpu_custom_call" | custom-call | tf_op jit(solution)/shard_map/pallas_call | solution.py:439
  37.4 1.8 %shard_map.95 = (f32[4,128,128]{2,1,0:T(8,128)}, f32[4,12,8,128]{3,2,1,0:T(8,128)}, f32[2,4,128]{2,1,0:T(4,128)}) custom-call(f32[4,128,128]{2,1,0:T(8,128)} %get-tuple-element.9.a_ref, f32[4,12,8,128]{3,2,1,0:T(8,128)} %get-tuple-element.10.b_ref, f32[2,4,128]{2,1,0:T(4,128)} %get-tuple-element.11.c_ref), custom_call_target="tpu_custom_call" | custom-call | tf_op jit(solution)/shard_map/pallas_call | solution.py:464
